TPU v7x, 512 devices: a whole 4x8x8 slice. The times are simulated.
512 devices in a mesh: freq: 128 (over z, y, core), panel: 4 (over x).
Axes of the slice: x: 4, y: 8, z: 8, core: 2. Of those that a mesh axis runs over, the one named last changes fastest.
Arguments:
- wave: bfloat16 [2, 128, 1600, 1600], P(None, 'freq', 'panel'), may hold values from -0.15625 to 0.15625
- observed: float32 [4, 6400, 512], P('panel', 'freq'), may hold values from -25 to 25
Outputs:
- solution: float32 [25600, 512], P('freq')
All inputs are finite; a program needn't handle non-finite values.
Results may differ from a plain program's by a relative error of at most 0.0085.
Values may be sent and summed in bfloat16 or wider, within the bound.
A program may use at most 64 MiB of HBM per device.

v0:
```python
import math
import jax
import jax.numpy as jnp
from jax import lax
from jax.sharding import PartitionSpec as P

VS = 16
ITERS = 3
SCALE = 0.5
precise = lax.Precision.HIGHEST
epsilon = 1e-06


def transform_tables(freq_total, samples):
    freq_index = lax.broadcasted_iota(jnp.int32, (freq_total, samples), 0) + 1
    time_index = lax.broadcasted_iota(jnp.int32, (freq_total, samples), 1)
    phases = (freq_index * time_index % samples).astype(jnp.float32) * (2.0 * math.pi / samples)
    factor = math.sqrt(2.0 / samples)
    return jnp.stack([factor * jnp.cos(phases), -factor * jnp.sin(phases)])


def two_parts(field):
    high = lax.reduce_precision(field, 8, 7)
    return jnp.concatenate([high, field - high]).astype(jnp.bfloat16)


def forward_product(model, wave):
    rows = two_parts(model.reshape(2 * VS, -1))

    def product_of(right):
        both = lax.dot_general(
            rows, right, (((1,), (1,)), ((), ())), preferred_element_type=jnp.float32
        )
        return both[: 2 * VS] + both[2 * VS :]

    by_real, by_imag = (product_of(wave[0]), product_of(wave[1]))
    return SCALE * jnp.stack([by_real[:VS] - by_imag[VS:], by_imag[:VS] + by_real[VS:]])


def adjoint_product(rows, wave):

    def product_of(right):
        both = jnp.dot(rows, right, preferred_element_type=jnp.float32)
        return both if rows.shape[0] == 2 * VS else both[: 2 * VS] + both[2 * VS :]

    by_real, by_imag = (product_of(wave[0]), product_of(wave[1]))
    return SCALE * jnp.stack([by_real[:VS] + by_imag[VS:], by_real[VS:] - by_imag[:VS]])


def iterate_weights(data_square, moments):
    model_norms = [jnp.sqrt(moments[2 * k]) for k in range(ITERS)]
    data_norms = [jnp.sqrt(data_square)] + [jnp.sqrt(moments[2 * k + 1]) for k in range(ITERS)]

    def ratio(top, bottom):
        return jnp.where(bottom > 0, top / jnp.where(bottom > 0, bottom, 1.0), 0.0)

    model_gram = [
        [ratio(ratio(moments[i + j], model_norms[i]), model_norms[j]) for j in range(ITERS)]
        for i in range(ITERS)
    ]

    def data_inner(i, j):
        low, high = (min(i, j), max(i, j))
        if high == 0:
            return data_square
        if low == 0:
            return moments[high - 1]
        return moments[low + high - 1]

    data_gram = [
        [ratio(ratio(data_inner(i, j), data_norms[i]), data_norms[j]) for j in range(ITERS + 1)]
        for i in range(ITERS + 1)
    ]

    def norm_of(weights, gram):
        total = 0.0
        for i in range(len(weights)):
            total += weights[i] * weights[i] * ratio(gram[i][i], gram[i][i])
            for j in range(i):
                total += 2.0 * weights[i] * weights[j] * gram[i][j]
        return jnp.sqrt(jnp.maximum(total, 0.0) + epsilon)

    up = [ratio(data_norms[k + 1], model_norms[k]) / SCALE for k in range(ITERS)]
    down = [ratio(model_norms[k], data_norms[k]) / SCALE for k in range(ITERS)]
    zero = jnp.zeros_like(data_square)
    beta = jnp.sqrt(data_square + epsilon)
    data_vector = [data_norms[0] / beta] + [zero] * ITERS
    model_vector = [data_vector[k] * down[k] for k in range(ITERS)]
    alpha = norm_of(model_vector, model_gram)
    model_vector = [weight / alpha for weight in model_vector]
    direction = model_vector
    solution = [zero] * ITERS
    phi_bar = beta
    rho_bar = alpha
    for step in range(ITERS):
        image = [zero] + [model_vector[k] * up[k] for k in range(ITERS)]
        data_vector = [new - alpha * old for new, old in zip(image, data_vector)]
        beta = norm_of(data_vector, data_gram)
        data_vector = [weight / beta for weight in data_vector]
        rho_new = jnp.sqrt(rho_bar * rho_bar + beta * beta)
        cosine = rho_bar / rho_new
        sine_part = beta / rho_new
        phi_value = cosine * phi_bar
        phi_bar = sine_part * phi_bar
        solution = [old + phi_value / rho_new * weight for old, weight in zip(solution, direction)]
        if step < ITERS - 1:
            image = [data_vector[k] * down[k] for k in range(ITERS)]
            model_vector = [new - beta * old for new, old in zip(image, model_vector)]
            alpha = norm_of(model_vector, model_gram)
            model_vector = [weight / alpha for weight in model_vector]
            theta = sine_part * alpha
            rho_bar = -cosine * alpha
            direction = [
                weight - theta / rho_new * old for weight, old in zip(model_vector, direction)
            ]
    return [ratio(weight, norm) for weight, norm in zip(solution, model_norms)]


def on_device(wave, observed):
    wave = wave[:, 0]
    panel_rows, sources = wave.shape[1:]
    blocks = lax.axis_size("freq")
    panels = lax.axis_size("panel")
    samples = observed.shape[2]
    table = transform_tables(blocks, samples)
    data = observed[0]

    def exchange(lines):
        return lax.all_to_all(lines, "freq", split_axis=0, concat_axis=0, tiled=True)

    lines = jnp.einsum("cft,rt->fcr", table, data, precision=precise).astype(jnp.bfloat16)
    moved_in = exchange(lines.reshape(-1)).reshape(blocks, 2, -1)
    rows = moved_in.transpose(1, 0, 2).reshape(2 * VS, panel_rows)
    bases, squares = ([], [jnp.sum(data * data)])
    for step in range(ITERS):
        model = lax.psum(adjoint_product(rows, wave), "panel")
        image = forward_product(model, wave)
        bases.append(model)
        squares += [jnp.sum(model * model) / panels, jnp.sum(image * image)]
        rows = two_parts(image.reshape(2 * VS, -1))
    squares = lax.psum(jnp.stack(squares), ("freq", "panel"))
    weights = iterate_weights(squares[0], [squares[1 + k] for k in range(2 * ITERS)])
    spectrum = sum((weight * basis for weight, basis in zip(weights, bases)))
    spectrum = spectrum.astype(jnp.bfloat16).reshape(2, blocks, -1)
    moved = exchange(spectrum.transpose(1, 0, 2).reshape(-1)).reshape(blocks, 2, -1)
    return jnp.einsum("jcr,cjt->rt", moved.astype(jnp.float32), table, precision=precise)


def solution(mesh):
    placed = (P(None, "freq", "panel", None), P("panel", "freq", None))
    return jax.shard_map(
        on_device, mesh=mesh, in_specs=placed, out_specs=P("freq", None), check_vma=False
    )
```

profile of v0, /device:TPU:1, one launch (start us, length us, event | category | flops | bytes accessed | tf_op | source)
XLA Modules:
  0.0 358.5 jit_solution(4462551454970142538)
XLA Ops:
  6.5 0.0 copy-start
  6.5 0.0 all-reduce.4.cloned.1.call-start
  6.5 1.1 cosine_multiply_fusion
  7.7 1.5 fusion.24
  9.2 0.1 copy.5
  9.3 29.7 %all_to_all.18 = bf16[128,100,1]{1,2,0:T(2,128)(2,1)S(1)} all-to-all(bf16[128,100,1]{1,2,0:T(2,128)(2,1)S(1)} %copy.5), channel_id=1, replica_groups=mesh['freq'=128,'panel'=4] {'freq'}, dimensions={0} | all-to-all | bytes 51200 | tf_op jit(solution)/shard_map/all_to_all | solution.py:129
  39.0 0.1 copy.6
  39.2 0.1 copy.7
  39.3 0.1 reshape.135
  39.4 1.7 fusion.10
  41.1 0.0 copy-done
  41.1 0.3 fusion.22
  41.5 0.7 maximum_multiply_fusion
  42.2 0.0 all-reduce.4.cloned.1.call-update
  42.2 0.0 all-reduce.6.cloned.1.call-start
  42.3 42.4 %all-reduce.4.cloned.1.call-done = f32[2,16,1600]{2,1,0:T(8,128)} async-done(((f32[2,16,1600]{2,1,0:T(8,128)}), f32[2,16,1600]{2,1,0:T(8,128)}) %all-reduce.4.cloned.1.call-update) | async-done | bytes 204816 | tf_op jit(solution)/shard_map/psum | solution.py:136
  84.6 1.0 reduce-precision_convert_fusion.2
  85.6 0.5 fusion.20
  86.1 0.5 fusion.8
  86.7 0.6 multiply_reduce_fusion.4
  87.3 0.0 copy-start.3
  87.3 0.4 fusion.18
  87.7 0.4 fusion.6
  88.1 0.7 maximum_multiply_fusion.1
  88.8 0.0 all-reduce.6.cloned.1.call-update
  88.9 0.0 all-reduce.8.cloned.1.call-start
  88.9 0.0 copy-done.3
  88.9 0.7 fusion.47
  89.6 51.8 %all-reduce.6.cloned.1.call-done = f32[2,16,1600]{2,1,0:T(8,128)} async-done(((f32[2,16,1600]{2,1,0:T(8,128)}), f32[2,16,1600]{2,1,0:T(8,128)}) %all-reduce.6.cloned.1.call-update) | async-done | bytes 204816 | tf_op jit(solution)/shard_map/psum | solution.py:136
  141.4 1.0 reduce-precision_convert_fusion.1
  142.3 0.5 fusion.16
  142.9 0.5 fusion.4
  143.5 0.6 multiply_reduce_fusion.3
  144.1 0.0 copy-start.1
  144.1 0.4 fusion.14
  144.5 0.4 fusion.2
  144.9 0.7 maximum_multiply_fusion.2
  145.6 0.0 all-reduce.8.cloned.1.call-update
  145.7 0.0 copy-done.1
  145.7 0.7 multiply_reduce_fusion.2
  146.9 1.7 multiply_reduce_fusion.1
  149.2 48.9 %all-reduce.8.cloned.1.call-done = f32[2,16,1600]{2,1,0:T(8,128)} async-done(((f32[2,16,1600]{2,1,0:T(8,128)}), f32[2,16,1600]{2,1,0:T(8,128)}) %all-reduce.8.cloned.1.call-update) | async-done | bytes 204816 | tf_op jit(solution)/shard_map/psum | solution.py:136
  198.1 0.0 copy-start.2
  198.1 1.0 reduce-precision_convert_fusion
  199.2 0.5 fusion.12
  199.7 0.5 fusion
  200.3 0.0 copy-done.2
  200.3 0.7 multiply_reduce_fusion
  201.6 0.7 fusion.58
  202.3 2.6 stack.109
  204.9 99.4 %psum.31 = f32[7]{0:T(128)S(1)} all-reduce(f32[7]{0:T(128)S(1)} %stack.109), channel_id=1, replica_groups=mesh['freq'=128,'panel'=4] {'freq','panel'}, use_global_device_ids=true, to_apply=%region_10.11 | all-reduce | flops 7 | bytes 56 | tf_op jit(solution)/shard_map/psum | solution.py:141
  304.2 0.7 fusion.77
  324.2 1.1 add_convert_fusion
  325.2 0.2 reshape.139
  325.5 0.1 copy.8
  325.6 0.2 copy.9
  325.8 0.5 broadcast.142
  326.3 1.4 reduce
  327.8 0.1 reshape.144
  327.9 22.6 %all_to_all.19 = bf16[128,2,200]{2,1,0:T(2,128)(2,1)S(1)} all-to-all(bf16[128,2,200]{2,1,0:T(2,128)(2,1)S(1)} %reshape.144), channel_id=1, replica_groups=mesh['freq'=128,'panel'=4] {'freq'}, dimensions={0} | all-to-all | bytes 204800 | tf_op jit(solution)/shard_map/all_to_all | solution.py:129
  350.5 0.2 reshape.145
  350.6 0.2 copy.10
  350.8 1.2 convolution_bitcast_fusion
  (20 shorter events, 0.4 us)
Async XLA Ops:
  6.5 34.5 %copy-start = (bf16[2,1,400,1600]{3,2,1,0:T(8,128)(2,1)S(1)}, bf16[2,1,400,1600]{3,2,1,0:T(8,128)(2,1)}, u32[]{:S(2)}) copy-start(bf16[2,1,400,1600]{3,2,1,0:T(8,128)(2,1)} %param.2) | copy-start | bytes 7680004
  6.5 78.1 %all-reduce.4.cloned.1.call-start = ((), (), s32[]{:S(2)}) async-start(), calls=%async_computation.2 | async-start | bytes 425984 | tf_op jit(solution)/shard_map/psum | solution.py:136
  42.2 99.2 %all-reduce.6.cloned.1.call-start = ((), (), s32[]{:S(2)}) async-start(), calls=%async_computation.3 | async-start | bytes 425984 | tf_op jit(solution)/shard_map/psum | solution.py:136
  87.3 1.6 copy-start.3
  88.9 109.3 %all-reduce.8.cloned.1.call-start = ((), (), s32[]{:S(2)}) async-start(), calls=%async_computation.4 | async-start | bytes 425984 | tf_op jit(solution)/shard_map/psum | solution.py:136
  144.1 1.6 copy-start.1
  198.1 2.1 copy-start.2
Sparse Core Ops, SparseCore 0:
  42.3 42.2 all-reduce.3
  89.0 52.3 all-reduce.5
  145.8 52.3 all-reduce.7
where the time goes:
time: 359 us; the launch traced here: 358 us
  blocking collectives  152 us (42%)
  waiting for transfers between devices  143 us (40%)
  between operations  34.6 us (10%)
  other arithmetic  14.6 us (4%)
  matrix products  9.22 us (3%)
  local copies, waits for them, and re-layouts  5.31 us (1%)
    psum x3, waiting for transfers between devices, on_device(): model = lax.psum(adjoint_product(rows, wave), 'panel')  143 us
    psum x1, blocking collectives, on_device(): squares = lax.psum(jnp.stack(squares), ('freq', 'panel'))  99.4 us
    all_to_all x2, blocking collectives, exchange(): lax.all_to_all(lines, 'freq', split_axis=0, concat_axis=0, tiled=True)  52.3 us
  transfers between devices with their start and end apart: 3, of which 3 were waited for; matrix products, arithmetic and copies ran while one was open for 1% of the time, Pallas kernels for 0%

commit v1 on v0

--- a/solution.py
+++ b/solution.py
@@ -133,7 +133,12 @@
     rows = moved_in.transpose(1, 0, 2).reshape(2 * VS, panel_rows)
     bases, squares = ([], [jnp.sum(data * data)])
     for step in range(ITERS):
-        model = lax.psum(adjoint_product(rows, wave), "panel")
+
+        def extend_the_members_all(z):
+            v_next = jnp.sum(lax.all_gather(z, axis_name="panel"), 0)
+            return v_next
+
+        model = extend_the_members_all(adjoint_product(rows, wave))
         image = forward_product(model, wave)
         bases.append(model)
         squares += [jnp.sum(model * model) / panels, jnp.sum(image * image)]

time: 359 us -> 236 us (0.66)
  waiting for transfers between devices: 143 us -> 9.87 us
  starting transfers between devices: 0.09 us -> 18.4 us
  between operations: 34.6 us -> 21.2 us
  blocking collectives: 152 us -> 156 us
    psum x3 -> x0, waiting for transfers between devices: 143 us -> none  [on_device(): model = lax.psum(adjoint_product(rows, wave), 'panel')]
    all_gather x0 -> x3, blocking collectives: none -> 34 us  [extend_the_members_all(): v_next = jnp.sum(lax.all_gather(z, axis_name='panel'), 0)]
    all_to_all x2 -> x1, blocking collectives: 52.3 us -> 19.9 us  [exchange(): lax.all_to_all(lines, 'freq', split_axis=0, concat_axis=0, tiled=True)]
    all_to_all x0 -> x1, starting transfers between devices: none -> 18.4 us  [exchange(): lax.all_to_all(lines, 'freq', split_axis=0, concat_axis=0, tiled=True)]
    all_to_all x0 -> x1, waiting for transfers between devices: none -> 9.87 us  [exchange(): lax.all_to_all(lines, 'freq', split_axis=0, concat_axis=0, tiled=True)]
  transfers between devices with their start and end apart: 3 -> 1, of which waited for: 3 -> 1; matrix products, arithmetic and copies ran while one was open for 1% -> 1% of each run, Pallas kernels for 0% -> 0%
where the time goes in v1:
time: 236 us; the launch traced here: 235 us
  blocking collectives  156 us (66%)
  between operations  21.2 us (9%)
  starting transfers between devices  18.4 us (8%)
  other arithmetic  13.8 us (6%)
  waiting for transfers between devices  9.87 us (4%)
  matrix products  9.21 us (4%)
  local copies, waits for them, and re-layouts  6.84 us (3%)
    psum x1, blocking collectives, on_device(): squares = lax.psum(jnp.stack(squares), ('freq', 'panel'))  102 us
    all_gather x3, blocking collectives, extend_the_members_all(): v_next = jnp.sum(lax.all_gather(z, axis_name='panel'), 0)  34 us
    all_to_all x1, blocking collectives, exchange(): lax.all_to_all(lines, 'freq', split_axis=0, concat_axis=0, tiled=True)  19.9 us
    all_to_all x1, starting transfers between devices, exchange(): lax.all_to_all(lines, 'freq', split_axis=0, concat_axis=0, tiled=True)  18.4 us
    all_to_all x1, waiting for transfers between devices, exchange(): lax.all_to_all(lines, 'freq', split_axis=0, concat_axis=0, tiled=True)  9.87 us
  transfers between devices with their start and end apart: 1, of which 1 were waited for; matrix products, arithmetic and copies ran while one was open for 1% of the time, Pallas kernels for 0%

profile of v1, /device:TPU:1, one launch (start us, length us, event | category | flops | bytes accessed | tf_op | source)
XLA Modules:
  0.0 235.2 jit_solution(12847054690980564816)
XLA Ops:
  0.0 1.1 cosine_multiply_fusion
  1.1 0.0 copy-start.4
  1.1 0.0 copy-start.6
  1.1 0.7 copy-done.4
  1.8 0.1 copy-done.6
  1.9 1.5 fusion.24
  3.4 0.7 copy.6
  4.2 18.4 %all-to-all-start = ((bf16[128,100,1]{1,2,0:T(2,128)(2,1)}), bf16[128,100,1]{1,2,0:T(2,128)(2,1)S(1)}, u32[]{:S(2)}, u32[]{:S(2)}) async-start(bf16[128,100,1]{1,2,0:T(2,128)(2,1)} %copy.6), calls=%async_computation | async-start | bytes 131072 | tf_op jit(solution)/shard_map/all_to_all | solution.py:129
  22.6 1.6 fusion.47
  24.2 9.9 %all-to-all-done = bf16[128,100,1]{1,2,0:T(2,128)(2,1)S(1)} async-done(((bf16[128,100,1]{1,2,0:T(2,128)(2,1)}), bf16[128,100,1]{1,2,0:T(2,128)(2,1)S(1)}, u32[]{:S(2)}, u32[]{:S(2)}) %all-to-all-start) | async-done | bytes 25632 | tf_op jit(solution)/shard_map/all_to_all | solution.py:129
  34.1 0.1 copy.7
  34.2 0.1 copy.8
  34.3 0.1 reshape.238
  34.4 1.7 fusion.10
  36.1 0.0 copy-done
  36.1 0.3 fusion.22
  36.5 12.3 %all_gather.12 = f32[4,2,16,1600]{3,2,1,0:T(8,128)S(1)} all-gather(f32[1,2,16,1600]{3,2,1,0:T(8,128)S(1)} %maximum_multiply_fusion), channel_id=1, replica_groups=mesh['freq'=128,'panel'=4] {'panel'}, dimensions={0}, use_global_device_ids=true | all-gather | bytes 1024000 | tf_op jit(solution)/shard_map/all_gather | solution.py:138
  48.8 0.7 reduce_sum.91
  49.5 1.0 reduce-precision_convert_fusion.2
  50.5 0.5 fusion.20
  51.0 0.5 fusion.8
  51.6 0.6 multiply_reduce_fusion.4
  52.3 0.4 fusion.18
  52.6 0.4 fusion.6
  53.1 10.6 %all_gather.13 = f32[4,2,16,1600]{3,2,1,0:T(8,128)S(1)} all-gather(f32[1,2,16,1600]{3,2,1,0:T(8,128)S(1)} %maximum_multiply_fusion.1), channel_id=1, replica_groups=mesh['freq'=128,'panel'=4] {'panel'}, dimensions={0}, use_global_device_ids=true | all-gather | bytes 1024000 | tf_op jit(solution)/shard_map/all_gather | solution.py:138
  63.7 0.7 reduce_sum.94
  64.4 1.0 reduce-precision_convert_fusion.1
  65.4 0.5 fusion.16
  65.9 0.5 fusion.4
  66.5 0.7 multiply_reduce_fusion.3
  67.2 0.4 fusion.14
  67.6 0.4 fusion.2
  68.1 11.1 %all_gather.14 = f32[4,2,16,1600]{3,2,1,0:T(8,128)S(1)} all-gather(f32[1,2,16,1600]{3,2,1,0:T(8,128)S(1)} %maximum_multiply_fusion.2), channel_id=1, replica_groups=mesh['freq'=128,'panel'=4] {'panel'}, dimensions={0}, use_global_device_ids=true | all-gather | bytes 1024000 | tf_op jit(solution)/shard_map/all_gather | solution.py:138
  79.2 0.7 reduce_sum.97
  79.9 0.0 copy-start.3
  79.9 0.0 copy-start.2
  79.9 0.0 copy-start.1
  79.9 1.0 reduce-precision_convert_fusion
  81.0 0.5 fusion.12
  81.5 0.5 fusion
  82.0 0.0 copy-done.3
  82.0 0.7 multiply_reduce_fusion
  82.7 0.0 copy-done.2
  82.7 0.0 copy-start.5
  82.7 0.0 copy-start.7
  82.7 0.7 multiply_reduce_fusion.1
  83.4 0.0 copy-done.1
  83.4 0.7 multiply_reduce_fusion.2
  86.1 0.7 fusion.58
  86.8 2.6 %stack.109 = f32[7]{0:T(128)S(1)} concatenate(f32[1]{0:T(128)} %bitcast, f32[1]{0:T(128)} %bitcast.7, f32[1]{0:T(128)} %bitcast.11, f32[1]{0:T(128)} %bitcast.15, f32[1]{0:T(128)} %bitcast.19, f32[1]{0:T(128)} %bitcast.23, f32[1]{0:T(128)} %bitcast.27), dimensions={0} | concatenate | bytes 56 | tf_op jit(solution)/shard_map/stack | solution.py:146
  89.5 102.2 %psum.7 = f32[7]{0:T(128)S(1)} all-reduce(f32[7]{0:T(128)S(1)} %stack.109), channel_id=1, replica_groups=mesh['freq'=128,'panel'=4] {'freq','panel'}, use_global_device_ids=true, to_apply=%region_10.11 | all-reduce | flops 7 | bytes 56 | tf_op jit(solution)/shard_map/psum | solution.py:146
  191.6 0.7 fusion.77
  211.2 0.2 convert_element_type.39
  211.4 0.1 copy.9
  211.5 0.2 copy.10
  211.7 0.6 broadcast.172
  212.3 1.4 reduce
  213.7 0.1 reshape.246
  213.9 19.9 %all_to_all.18 = bf16[128,2,200]{2,1,0:T(2,128)(2,1)S(1)} all-to-all(bf16[128,2,200]{2,1,0:T(2,128)(2,1)S(1)} %reshape.246), channel_id=1, replica_groups=mesh['freq'=128,'panel'=4] {'freq'}, dimensions={0} | all-to-all | bytes 204800 | tf_op jit(solution)/shard_map/all_to_all | solution.py:129
  233.7 0.2 reshape.247
  233.9 0.2 copy.11
  234.1 0.0 copy-done.5
  234.1 0.0 copy-done.7
  234.1 1.1 convolution_bitcast_fusion
  (25 shorter events, 0.4 us)
Async XLA Ops:
  0.0 36.1 %copy-start = (bf16[2,1,400,1600]{3,2,1,0:T(8,128)(2,1)S(1)}, bf16[2,1,400,1600]{3,2,1,0:T(8,128)(2,1)}, u32[]{:S(2)}) copy-start(bf16[2,1,400,1600]{3,2,1,0:T(8,128)(2,1)} %param.2) | copy-start | bytes 7680004
  1.1 0.7 copy-start.4
  1.1 0.8 copy-start.6
  4.2 29.9 %all-to-all-start = ((bf16[128,100,1]{1,2,0:T(2,128)(2,1)}), bf16[128,100,1]{1,2,0:T(2,128)(2,1)S(1)}, u32[]{:S(2)}, u32[]{:S(2)}) async-start(bf16[128,100,1]{1,2,0:T(2,128)(2,1)} %copy.6), calls=%async_computation | async-start | bytes 131072 | tf_op jit(solution)/shard_map/all_to_all | solution.py:129
  79.9 2.1 copy-start.3
  79.9 2.8 %copy-start.2 = (f32[2,16,1600]{2,1,0:T(8,128)S(1)}, f32[2,16,1600]{2,1,0:T(8,128)}, u32[]{:S(2)}) copy-start(f32[2,16,1600]{2,1,0:T(8,128)} %reduce_sum.94) | copy-start | bytes 614404
  79.9 3.5 %copy-start.1 = (f32[2,16,1600]{2,1,0:T(8,128)S(1)}, f32[2,16,1600]{2,1,0:T(8,128)}, u32[]{:S(2)}) copy-start(f32[2,16,1600]{2,1,0:T(8,128)} %reduce_sum.91) | copy-start | bytes 614404
  82.7 151.4 %copy-start.5 = (f32[1,128,512]{2,1,0:T(8,128)S(1)}, f32[1,128,512]{2,1,0:T(8,128)}, u32[]{:S(2)}) copy-start(f32[1,128,512]{2,1,0:T(8,128)} %copy-done.4) | copy-start | bytes 786436
  82.7 151.4 %copy-start.7 = (f32[1,128,512]{2,1,0:T(8,128)S(1)}, f32[1,128,512]{2,1,0:T(8,128)}, u32[]{:S(2)}) copy-start(f32[1,128,512]{2,1,0:T(8,128)} %copy-done.6) | copy-start | bytes 786436
